TPU v7x, 32 devices: a whole 2x2x4 slice. The times are simulated.
32 devices in a mesh: grp: 4 (over x, core), mem: 8 (over z, y).
Axes of the slice: x: 2, y: 2, z: 4, core: 2. Of those that a mesh axis runs over, the one named last changes fastest.
Arguments:
- features: bfloat16 [32768, 4096], P(('grp', 'mem')), may hold values from -0.09375 to 0.09375
- re_features: bfloat16 [32768, 256], P(('grp', 'mem')), may hold values from -6 to 6
- member_id: int32 [32768], P(('grp', 'mem')), may hold values from 0 to 255, as said below
- slot: int32 [32768], P(('grp', 'mem')), may hold values from 0 to 2047, as said below
- labels: int32 [32768], P(('grp', 'mem')), may hold values 0 or 1
- offsets: float32 [32768], P(('grp', 'mem')), may hold values from -6 to 6
- feature_scale: float32 [4096], replicated, may hold values from 0.3 to 3
- w_start: float32 [4096], replicated, may hold values from -4 to 4
Outputs:
- fixed_weights: float32 [4096], replicated
- member_coef: float32 [256, 256], P(('grp', 'mem'))
- row_offsets: float32 [32768], P(('grp', 'mem'))
Inputs may be any that keep to these rules, and one draw needn't show every extreme that they name: A row of device k (devices counted along grp, then mem) belongs to group k // 8: member_id // 64 is that group, and (member_id mod 64) // 8 equals slot // 256. Rows per member are uneven. Within one device's rows the slots are distinct; slot // 256 is the mem index that owns the row's member, so at most 256 rows of one device go to one owner, and in every group one owner receives exactly 256 rows from every device of the group.
All inputs are finite; a program needn't handle non-finite values. No bound on the sum of `labels` on one device may be relied on, other than what follows from the above.
Results may differ from a plain program's by a relative error of at most 0.0003.
Values may be sent and summed in bfloat16 or wider, within the bound.
A program may use at most 64 MiB of HBM per device.

v0:
```python
import jax
import jax.numpy as jnp
from jax import lax
from jax.sharding import PartitionSpec as P

MEM_DEV = 8
NEWTON = 2
CG_ITERS = 3
ridge_fixed = 1.0
ridge_member = 1.0


def split_pair(values):
    upper_part = values.astype(jnp.bfloat16)
    held_part = lax.optimization_barrier(upper_part)
    lower_part = (values - held_part.astype(jnp.float32)).astype(jnp.bfloat16)
    return (upper_part, lower_part)


def split_two(vector):
    upper_part, lower_part = split_pair(vector)
    return jnp.stack([upper_part, lower_part], axis=1)


def apply_rows(features, vector):
    return jnp.sum(jnp.dot(features, split_two(vector), preferred_element_type=jnp.float32), axis=1)


def apply_columns(features, values):
    pair_cols = split_two(values)
    product = lax.dot_general(
        pair_cols, features, (((0,), (0,)), ((), ())), preferred_element_type=jnp.float32
    )
    return jnp.sum(product, axis=0)


def inner_rows(left, right):
    return lax.dot_general(
        left, right, (((0,), (0,)), ((), ())), preferred_element_type=jnp.float32
    )


def hessian_times(features, feature_scale, curvature, direction):
    inner = curvature * apply_rows(features, feature_scale * direction)
    summed = lax.psum(apply_columns(features, inner), ("grp", "mem"))
    return feature_scale * summed + ridge_fixed * direction


def fit_members(received, arrived):
    curv_row = arrived[0]
    resid_row = arrived[1]
    local_row = arrived[2]
    onehot = (local_row[:, None] == jnp.arange(MEM_DEV).astype(arrived.dtype)[None, :]).astype(
        arrived.dtype
    )
    z_float = received.astype(jnp.float32)

    def gram_one(column):
        upper_part, lower_part = split_pair(z_float * (curv_row * column)[:, None])
        return inner_rows(received, upper_part) + inner_rows(received, lower_part)

    gram_all = lax.map(gram_one, onehot.T) + ridge_member * jnp.eye(
        received.shape[1], dtype=jnp.float32
    )
    grad_upper, grad_lower = split_pair(resid_row[:, None] * onehot)
    member_grad = inner_rows(grad_upper, received) + inner_rows(grad_lower, received)
    factor = jnp.linalg.cholesky(gram_all)
    member_coef = -jax.scipy.linalg.cho_solve((factor, True), member_grad[:, :, None])[:, :, 0]
    coef_upper, coef_lower = split_pair(member_coef)
    scores = jnp.dot(received, coef_upper.T, preferred_element_type=jnp.float32) + jnp.dot(
        received, coef_lower.T, preferred_element_type=jnp.float32
    )
    return (member_coef, jnp.sum(scores * onehot, axis=1))


def on_device(features, re_features, member_id, slot, labels, offsets, feature_scale, w_start):
    row_count = features.shape[0]
    slots_all = 2 * row_count
    packed = jnp.zeros((slots_all, re_features.shape[1]), jnp.bfloat16).at[slot].set(re_features)
    received = None
    target = labels.astype(jnp.float32)
    weights = w_start
    for newton_step in range(NEWTON):
        margin = apply_rows(features, feature_scale * weights) + offsets
        probability = jax.nn.sigmoid(margin)
        curvature = probability * (1.0 - probability)
        summed = lax.psum(apply_columns(features, probability - target), ("grp", "mem"))
        gradient = feature_scale * summed + ridge_fixed * weights
        residual = -gradient
        direction = residual
        res_norm = jnp.sum(residual * residual)
        update = jnp.zeros_like(weights)
        for cg_step in range(CG_ITERS):
            hess_image = hessian_times(features, feature_scale, curvature, direction)
            step_size = res_norm / jnp.sum(direction * hess_image)
            update = update + step_size * direction
            residual = residual - step_size * hess_image
            next_norm = jnp.sum(residual * residual)
            direction = residual + next_norm / res_norm * direction
            res_norm = next_norm
        weights = weights + update
    score = apply_rows(features, feature_scale * weights)
    probability = jax.nn.sigmoid(score)
    curvature = probability * (1.0 - probability)
    resid_row = probability - target
    local_id = (member_id % MEM_DEV).astype(jnp.float32)
    row_weights = jnp.stack([curvature, resid_row, local_id], axis=0)
    weight_slots = jnp.zeros((3, slots_all), jnp.float32).at[:, slot].set(row_weights)
    received = lax.all_to_all(packed, "mem", split_axis=0, concat_axis=0, tiled=True)
    arrived = lax.all_to_all(weight_slots, "mem", split_axis=1, concat_axis=1, tiled=True)
    member_coef, slot_scores = fit_members(received, arrived)
    returned = lax.all_to_all(slot_scores, "mem", split_axis=0, concat_axis=0, tiled=True)
    row_offsets = returned[slot]
    return (weights, member_coef, row_offsets)


def solution(mesh):
    placed = (
        P(("grp", "mem"), None),
        P(("grp", "mem"), None),
        P(("grp", "mem")),
        P(("grp", "mem")),
        P(("grp", "mem")),
        P(("grp", "mem")),
        P(),
        P(),
    )
    return jax.shard_map(
        on_device,
        mesh=mesh,
        in_specs=placed,
        out_specs=(P(), P(("grp", "mem"), None), P(("grp", "mem"))),
        check_vma=False,
    )
```

profile of v0, /device:TPU:0, one launch (start us, length us, event | category | flops | bytes accessed | tf_op | source)
XLA Modules:
  0.0 981.4 jit_solution(12740496581098813807)
XLA Ops:
  1.5 5.8 convolution_reduce_fusion.16
  8.6 42.1 %psum.56 = f32[4096]{0:T(1024)S(1)} all-reduce(f32[4096]{0:T(1024)S(1)} %convolution_reduce_fusion.7), channel_id=1, replica_groups=mesh['grp'=4,'mem'=8] {'grp','mem'}, use_global_device_ids=true, to_apply=%region_2.0 | all-reduce | flops 4096 | bytes 32768 | tf_op jit(solution)/shard_map/psum | solution.py:87
  50.8 5.8 convolution_reduce_fusion.15
  57.9 40.2 %psum.57 = f32[4096]{0:T(1024)S(1)} all-reduce(f32[4096]{0:T(1024)S(1)} %convolution_reduce_fusion.6), channel_id=1, replica_groups=mesh['grp'=4,'mem'=8] {'grp','mem'}, use_global_device_ids=true, to_apply=%region_6.0 | all-reduce | flops 4096 | bytes 32768 | tf_op jit(solution)/shard_map/psum | solution.py:45
  102.1 5.7 convolution_reduce_fusion.14
  112.4 40.2 %psum.58 = f32[4096]{0:T(1024)S(1)} all-reduce(f32[4096]{0:T(1024)S(1)} %convolution_reduce_fusion.5), channel_id=1, replica_groups=mesh['grp'=4,'mem'=8] {'grp','mem'}, use_global_device_ids=true, to_apply=%region_11.0 | all-reduce | flops 4096 | bytes 32768 | tf_op jit(solution)/shard_map/psum | solution.py:45
  166.9 40.2 %psum.59 = f32[4096]{0:T(1024)S(1)} all-reduce(f32[4096]{0:T(1024)S(1)} %convolution_reduce_fusion.4), channel_id=1, replica_groups=mesh['grp'=4,'mem'=8] {'grp','mem'}, use_global_device_ids=true, to_apply=%region_16.0 | all-reduce | flops 4096 | bytes 32768 | tf_op jit(solution)/shard_map/psum | solution.py:45
  219.5 40.1 %psum.60 = f32[4096]{0:T(1024)S(1)} all-reduce(f32[4096]{0:T(1024)S(1)} %convolution_reduce_fusion.3), channel_id=1, replica_groups=mesh['grp'=4,'mem'=8] {'grp','mem'}, use_global_device_ids=true, to_apply=%region_20.0 | all-reduce | flops 4096 | bytes 32768 | tf_op jit(solution)/shard_map/psum | solution.py:87
  269.9 40.7 %psum.61 = f32[4096]{0:T(1024)S(1)} all-reduce(f32[4096]{0:T(1024)S(1)} %convolution_reduce_fusion.2), channel_id=1, replica_groups=mesh['grp'=4,'mem'=8] {'grp','mem'}, use_global_device_ids=true, to_apply=%region_24.0 | all-reduce | flops 4096 | bytes 32768 | tf_op jit(solution)/shard_map/psum | solution.py:45
  314.5 5.7 convolution_reduce_fusion.10
  324.8 39.9 %psum.62 = f32[4096]{0:T(1024)S(1)} all-reduce(f32[4096]{0:T(1024)S(1)} %convolution_reduce_fusion.1), channel_id=1, replica_groups=mesh['grp'=4,'mem'=8] {'grp','mem'}, use_global_device_ids=true, to_apply=%region_29.0 | all-reduce | flops 4096 | bytes 32768 | tf_op jit(solution)/shard_map/psum | solution.py:45
  368.7 5.7 convolution_reduce_fusion.9
  379.1 40.3 %psum.63 = f32[4096]{0:T(1024)S(1)} all-reduce(f32[4096]{0:T(1024)S(1)} %convolution_reduce_fusion), channel_id=1, replica_groups=mesh['grp'=4,'mem'=8] {'grp','mem'}, use_global_device_ids=true, to_apply=%region_34.0 | all-reduce | flops 4096 | bytes 32768 | tf_op jit(solution)/shard_map/psum | solution.py:45
  438.2 6.4 scatter_custom_fusion.1
  444.9 5.7 all-to-all-start.1
  453.3 22.0 %all-to-all-done.1 = bf16[8,256,256]{2,1,0:T(8,128)(2,1)S(1)} async-done(((bf16[8,256,256]{2,1,0:T(8,128)(2,1)}), bf16[8,256,256]{2,1,0:T(8,128)(2,1)S(1)}, u32[]{:S(2)}, u32[]{:S(2)}) %all-to-all-start.1) | async-done | bytes 1048608 | tf_op jit(solution)/shard_map/all_to_all | solution.py:109
  476.4 19.9 %while.11 = (s32[]{:T(128)}, f32[8,256,256]{1,2,0:T(8,128)}, f32[8,2048]{1,0:T(8,128)S(1)}, f32[2048]{0:T(1024)S(1)}, f32[2048,256]{1,0:T(8,128)S(1)}, /*index=5*/bf16[2048,256]{1,0:T(8,128)(2,1)S(1)}, s32[]{:T(128)}) while((s32[]{:T(128)}, f32[8,256,256]{1,2,0:T(8,128)}, f32[8,2048]{1,0:T(8,128)S(1)}, f32[2048]{0:T(1024)S(1)}, ...), condition=%wide.region_40.41_spmd, body=%wide.region_39.40_spmd.sunk | while | flops 540084224 | bytes 10281053 | solution.py:62
  505.7 94.4 %custom-call.20 = f32[8,128,128]{2,1,0:T(8,128)} custom-call(f32[8,128,128]{2,1,0:T(8,128)S(1)} %cholesky.119), custom_call_target="Cholesky" | custom-call | tf_op jit(solution)/shard_map/jit(cholesky)/cholesky | solution.py:67
  602.3 80.0 %custom-call.21 = f32[8,1,128,128]{2,3,1,0:T(8,128)} custom-call(f32[8,1,128,128]{3,2,1,0:T(8,128)} %select_bitcast_fusion), custom_call_target="InvertDiagBlocksLowerTriangular" | custom-call | tf_op jit(solution)/shard_map/jit(cholesky)/cholesky | solution.py:67
  687.3 95.4 %custom-call.22 = f32[8,128,128]{2,1,0:T(8,128)} custom-call(f32[8,128,128]{2,1,0:T(8,128)} %convolution_subtract_fusion), custom_call_target="Cholesky" | custom-call | tf_op jit(solution)/shard_map/jit(cholesky)/cholesky | solution.py:67
  787.8 5.9 while.12
  793.7 158.7 %custom-call.23 = f32[8,2,128,128]{2,3,1,0:T(8,128)} custom-call(f32[8,2,128,128]{3,2,1,0:T(8,128)} %bitcast.163), custom_call_target="InvertDiagBlocksLowerTriangular" | custom-call | tf_op jit(solution)/shard_map/jit(_cho_solve)/vmap()/triangular_solve | solution.py:68
  960.9 9.7 all_to_all.33
  970.6 10.5 %gather_fusion = f32[1024]{0:T(1024)} fusion(f32[2048]{0:T(1024)S(1)} %bitcast.135, s32[1024]{0:T(1024)S(1)} %copy-done.20), kind=kCustom, calls=%fused_computation | custom fusion | bytes 12288 | tf_op jit(solution)/shard_map/gather | solution.py:113
  (238 shorter events, 130.7 us)
Async XLA Ops:
  1.4 5.9 copy-start.12
  1.4 5.9 copy-start.19
  1.4 5.9 copy-start
  7.4 43.3 %copy-start.4 = (f32[4096]{0:T(1024)S(1)}, f32[4096]{0:T(1024)}, u32[]{:S(2)}) copy-start(f32[4096]{0:T(1024)} %param.16) | copy-start | bytes 49156
  7.4 43.3 %copy-start.8 = (f32[4096]{0:T(1024)S(1)}, f32[4096]{0:T(1024)}, u32[]{:S(2)}) copy-start(f32[4096]{0:T(1024)} %param.17) | copy-start | bytes 49156
  50.8 5.9 copy-start.1
  374.5 47.5 %copy-start.23 = (s32[1024]{0:T(1024)S(1)}, s32[1024]{0:T(1024)}, u32[]{:S(2)}) copy-start(s32[1024]{0:T(1024)} %param.13) | copy-start | bytes 12292
  374.5 48.1 %copy-start.24 = (s32[1024]{0:T(1024)S(1)}, s32[1024]{0:T(1024)}, u32[]{:S(2)}) copy-start(s32[1024]{0:T(1024)} %param.12) | copy-start | bytes 12292
  433.0 11.9 %all-to-all-start = ((f32[3,8,256]{2,0,1:T(4,128)}), f32[3,8,256]{2,0,1:T(4,128)S(1)}, u32[]{:S(2)}, u32[]{:S(2)}) async-start(f32[3,8,256]{2,0,1:T(4,128)} %copy.32), calls=%async_computation | async-start | bytes 65536 | tf_op jit(solution)/shard_map/all_to_all | solution.py:110
  444.9 30.4 %all-to-all-start.1 = ((bf16[8,256,256]{2,1,0:T(8,128)(2,1)}), bf16[8,256,256]{2,1,0:T(8,128)(2,1)S(1)}, u32[]{:S(2)}, u32[]{:S(2)}) async-start(bf16[8,256,256]{2,1,0:T(8,128)(2,1)} %bitcast.10), calls=%async_computation.1 | async-start | bytes 2097152 | tf_op jit(solution)/shard_map/all_to_all | solution.py:109
  450.7 24.6 %copy-start.21 = (f32[8]{0:T(128)}, f32[8]{0:T(128)S(1)}, u32[]{:S(2)}) copy-start(f32[8]{0:T(128)S(1)} %iota_convert_fusion) | copy-start | bytes 100
  452.5 22.8 %copy-start.9 = (f32[1,8,256]{2,0,1:T(1,128)}, f32[1,8,256]{2,0,1:T(1,128)S(1)}, u32[]{:S(2)}) copy-start(f32[1,8,256]{2,0,1:T(1,128)S(1)} %get-tuple-element.123) | copy-start | bytes 24580
  505.7 95.8 %copy-start.14 = (pred[128,128]{1,0:T(8,128)(4,1)S(1)}, pred[128,128]{1,0:T(8,128)(4,1)}, u32[]{:S(2)}) copy-start(pred[128,128]{1,0:T(8,128)(4,1)} %iota_compare_fusion.2) | copy-start | bytes 49156
  682.4 100.4 %copy-start.10 = (f32[1,8,256]{2,0,1:T(1,128)S(1)}, f32[1,8,256]{2,0,1:T(1,128)}, u32[]{:S(2)}) copy-start(f32[1,8,256]{2,0,1:T(1,128)} %copy-done.9) | copy-start | bytes 24580
  682.4 100.4 %copy-start.11 = (bf16[2048,8]{0,1:T(8,128)(2,1)S(1)}, bf16[2048,8]{0,1:T(8,128)(2,1)}, u32[]{:S(2)}) copy-start(bf16[2048,8]{0,1:T(8,128)(2,1)} %select_convert_fusion) | copy-start | bytes 98308
  682.4 100.4 %copy-start.15 = (f32[8,256]{1,0:T(8,128)S(1)}, f32[8,256]{1,0:T(8,128)}, u32[]{:S(2)}) copy-start(f32[8,256]{1,0:T(8,128)} %fusion.128) | copy-start | bytes 24580
  682.4 100.4 %copy-start.22 = (f32[8]{0:T(128)S(1)}, f32[8]{0:T(128)}, u32[]{:S(2)}) copy-start(f32[8]{0:T(128)} %copy-done.21) | copy-start | bytes 100
  684.3 98.8 %copy-start.13 = (pred[128,128]{1,0:T(8,128)(4,1)S(1)}, pred[128,128]{1,0:T(8,128)(4,1)}, u32[]{:S(2)}) copy-start(pred[128,128]{1,0:T(8,128)(4,1)} %iota_compare_fusion.3) | copy-start | bytes 49156
  783.1 4.6 copy-start.16
  787.8 164.6 %slice-start = ((f32[8,256,1]{1,0,2:T(8,128)}), f32[8,128,1]{1,0,2:T(8,128)S(1)}, s32[]{:S(2)}) async-start(f32[8,256,1]{1,0,2:T(8,128)} %copy-done.16), calls=%async_computation.3 | async-start | bytes 8192 | tf_op jit(solution)/shard_map/jit(_cho_solve)/vmap()/triangular_solve | solution.py:68
  787.8 167.2 %copy-start.17 = (f32[8,256,1]{1,0,2:T(8,128)S(1)}, f32[8,256,1]{1,0,2:T(8,128)}, u32[]{:S(2)}) copy-start(f32[8,256,1]{1,0,2:T(8,128)} %copy-done.16) | copy-start | bytes 24580
  952.4 6.8 copy-start.7
  956.6 14.0 %copy-start.20 = (s32[1024]{0:T(1024)S(1)}, s32[1024]{0:T(1024)}, u32[]{:S(2)}) copy-start(s32[1024]{0:T(1024)} %get-tuple-element.126) | copy-start | bytes 12292
  960.1 21.1 %copy-start.18 = (f32[8,256]{1,0:T(8,128)}, f32[8,256]{1,0:T(8,128)S(1)}, u32[]{:S(2)}) copy-start(f32[8,256]{1,0:T(8,128)S(1)} %get-tuple-element.95) | copy-start | bytes 24580
  (5 other events, 9.0 us)
where the time goes:
time: 991 us; the launch traced here: 981 us
  other arithmetic  452 us (46%)
  blocking collectives  333 us (34%)
  matrix products  113 us (11%)
  local copies, waits for them, and re-layouts  35 us (4%)
  waiting for transfers between devices  22.3 us (2%)
  between operations  15.2 us (2%)
  starting transfers between devices  10.9 us (1%)
    another operation x9, other arithmetic, fit_members(): factor = jnp.linalg.cholesky(gram_all)  273 us
    psum x6, blocking collectives, hessian_times(): summed = lax.psum(apply_columns(features, inner), ('grp', 'mem'))  241 us
    another operation x6, other arithmetic, fit_members(): jax.scipy.linalg.cho_solve((factor, True), member_grad[:, :, None])[:, :, 0]  161 us
    psum x2, blocking collectives, on_device(): lax.psum(apply_columns(features, probability - target), ('grp', 'mem'))  82.1 us
    dot_general x9, matrix products, apply_rows(): jnp.dot(features, split_two(vector), preferred_element_type=jnp.float32)  51.3 us
    dot_general x8, matrix products, apply_columns(): lax.dot_general(pair_cols, features, (((0,), (0,)), ((), ())), preferred_...  29.9 us
    all_to_all x1, waiting for transfers between devices, on_device(): lax.all_to_all(packed, 'mem', split_axis=0, concat_axis=0, tiled=True)  22 us
  transfers between devices with their start and end apart: 2, of which 2 were waited for; matrix products, arithmetic and copies ran while one was open for 1% of the time, Pallas kernels for 0%

commit v1 on v0

--- a/solution.py
+++ b/solution.py
@@ -42,7 +42,9 @@
 
 def hessian_times(features, feature_scale, curvature, direction):
     inner = curvature * apply_rows(features, feature_scale * direction)
-    summed = lax.psum(apply_columns(features, inner), ("grp", "mem"))
+    own = apply_columns(features, inner)
+    parts = lax.all_gather(own, ("grp", "mem"), axis=0, tiled=False)
+    summed = parts.sum(axis=0)
     return feature_scale * summed + ridge_fixed * direction
 
 

time: 991 us -> 1150 us (1.16)
  blocking collectives: 333 us -> 498 us
    all_gather x0 -> x6, blocking collectives: none -> 409 us  [hessian_times(): parts = lax.all_gather(own, ('grp', 'mem'), axis=0, tiled=False)]
    psum x6 -> x0, blocking collectives: 241 us -> none  [hessian_times(): summed = lax.psum(apply_columns(features, inner), ('grp', 'mem'))]
where the time goes in v1:
time: 1150 us; the launch traced here: 1140 us
  blocking collectives  498 us (43%)
  other arithmetic  452 us (39%)
  matrix products  113 us (10%)
  local copies, waits for them, and re-layouts  35.4 us (3%)
  waiting for transfers between devices  20.8 us (2%)
  between operations  15.2 us (1%)
    all_gather x6, blocking collectives, hessian_times(): parts = lax.all_gather(own, ('grp', 'mem'), axis=0, tiled=False)  409 us
    another operation x9, other arithmetic, fit_members(): factor = jnp.linalg.cholesky(gram_all)  273 us
    another operation x6, other arithmetic, fit_members(): jax.scipy.linalg.cho_solve((factor, True), member_grad[:, :, None])[:, :, 0]  161 us
    psum x2, blocking collectives, on_device(): lax.psum(apply_columns(features, probability - target), ('grp', 'mem'))  79 us
    dot_general x9, matrix products, apply_rows(): jnp.dot(features, split_two(vector), preferred_element_type=jnp.float32)  51.3 us
    dot_general x8, matrix products, apply_columns(): lax.dot_general(pair_cols, features, (((0,), (0,)), ((), ())), preferred_...  29.9 us
  transfers between devices with their start and end apart: 2, of which 2 were waited for; matrix products, arithmetic and copies ran while one was open for 1% of the time, Pallas kernels for 0%

profile of v1, /device:TPU:0, one launch (start us, length us, event | category | flops | bytes accessed | tf_op | source)
XLA Modules:
  0.0 1144.0 jit_solution(18255535297157110058)
XLA Ops:
  1.5 5.8 convolution_reduce_fusion.16
  8.6 42.1 %psum.14 = f32[4096]{0:T(1024)S(1)} all-reduce(f32[4096]{0:T(1024)S(1)} %convolution_reduce_fusion.7), channel_id=1, replica_groups=mesh['grp'=4,'mem'=8] {'grp','mem'}, use_global_device_ids=true, to_apply=%region_2.0 | all-reduce | flops 4096 | bytes 32768 | tf_op jit(solution)/shard_map/psum | solution.py:89
  50.8 5.8 convolution_reduce_fusion.15
  57.9 69.0 %all-gather = f32[131072]{0:T(1024)S(1)} all-gather(f32[4096]{0:T(1024)S(1)} %convolution_reduce_fusion.6), channel_id=2, replica_groups=mesh['grp'=4,'mem'=8] {'grp','mem'}, dimensions={0}, use_global_device_ids=true | all-gather | bytes 540672 | tf_op jit(solution)/shard_map/all_gather | solution.py:46
  131.0 5.7 convolution_reduce_fusion.14
  141.3 66.8 %all-gather.1 = f32[131072]{0:T(1024)S(1)} all-gather(f32[4096]{0:T(1024)S(1)} %convolution_reduce_fusion.5), channel_id=3, replica_groups=mesh['grp'=4,'mem'=8] {'grp','mem'}, dimensions={0}, use_global_device_ids=true | all-gather | bytes 540672 | tf_op jit(solution)/shard_map/all_gather | solution.py:46
  222.6 69.2 %all-gather.2 = f32[131072]{0:T(1024)S(1)} all-gather(f32[4096]{0:T(1024)S(1)} %convolution_reduce_fusion.4), channel_id=4, replica_groups=mesh['grp'=4,'mem'=8] {'grp','mem'}, dimensions={0}, use_global_device_ids=true | all-gather | bytes 540672 | tf_op jit(solution)/shard_map/all_gather | solution.py:46
  294.0 5.7 convolution_reduce_fusion.12
  304.3 36.9 %psum.15 = f32[4096]{0:T(1024)S(1)} all-reduce(f32[4096]{0:T(1024)S(1)} %convolution_reduce_fusion.3), channel_id=1, replica_groups=mesh['grp'=4,'mem'=8] {'grp','mem'}, use_global_device_ids=true, to_apply=%region_20.0 | all-reduce | flops 4096 | bytes 32768 | tf_op jit(solution)/shard_map/psum | solution.py:89
  341.3 5.7 convolution_reduce_fusion.11
  351.6 69.3 %all-gather.3 = f32[131072]{0:T(1024)S(1)} all-gather(f32[4096]{0:T(1024)S(1)} %convolution_reduce_fusion.2), channel_id=5, replica_groups=mesh['grp'=4,'mem'=8] {'grp','mem'}, dimensions={0}, use_global_device_ids=true | all-gather | bytes 540672 | tf_op jit(solution)/shard_map/all_gather | solution.py:46
  435.4 66.6 %all-gather.4 = f32[131072]{0:T(1024)S(1)} all-gather(f32[4096]{0:T(1024)S(1)} %convolution_reduce_fusion.1), channel_id=6, replica_groups=mesh['grp'=4,'mem'=8] {'grp','mem'}, dimensions={0}, use_global_device_ids=true | all-gather | bytes 540672 | tf_op jit(solution)/shard_map/all_gather | solution.py:46
  516.5 68.5 %all-gather.5 = f32[131072]{0:T(1024)S(1)} all-gather(f32[4096]{0:T(1024)S(1)} %convolution_reduce_fusion), channel_id=7, replica_groups=mesh['grp'=4,'mem'=8] {'grp','mem'}, dimensions={0}, use_global_device_ids=true | all-gather | bytes 540672 | tf_op jit(solution)/shard_map/all_gather | solution.py:46
  602.4 6.4 scatter_custom_fusion.1
  609.0 5.8 all-to-all-start.1
  617.4 20.6 %all-to-all-done.1 = bf16[8,256,256]{2,1,0:T(8,128)(2,1)S(1)} async-done(((bf16[8,256,256]{2,1,0:T(8,128)(2,1)}), bf16[8,256,256]{2,1,0:T(8,128)(2,1)S(1)}, u32[]{:S(2)}, u32[]{:S(2)}) %all-to-all-start.1) | async-done | bytes 1048608 | tf_op jit(solution)/shard_map/all_to_all | solution.py:111
  639.1 19.9 %while.11 = (s32[]{:T(128)}, f32[8,256,256]{1,2,0:T(8,128)}, f32[8,2048]{1,0:T(8,128)S(1)}, f32[2048]{0:T(1024)S(1)}, f32[2048,256]{1,0:T(8,128)S(1)}, /*index=5*/bf16[2048,256]{1,0:T(8,128)(2,1)S(1)}, s32[]{:T(128)}) while((s32[]{:T(128)}, f32[8,256,256]{1,2,0:T(8,128)}, f32[8,2048]{1,0:T(8,128)S(1)}, f32[2048]{0:T(1024)S(1)}, ...), condition=%wide.region_40.41_spmd, body=%wide.region_39.40_spmd.sunk | while | flops 540084224 | bytes 10281053 | solution.py:64
  668.4 94.4 %custom-call.20 = f32[8,128,128]{2,1,0:T(8,128)} custom-call(f32[8,128,128]{2,1,0:T(8,128)S(1)} %cholesky.119), custom_call_target="Cholesky" | custom-call | tf_op jit(solution)/shard_map/jit(cholesky)/cholesky | solution.py:69
  765.0 80.0 %custom-call.21 = f32[8,1,128,128]{2,3,1,0:T(8,128)} custom-call(f32[8,1,128,128]{3,2,1,0:T(8,128)} %select_bitcast_fusion), custom_call_target="InvertDiagBlocksLowerTriangular" | custom-call | tf_op jit(solution)/shard_map/jit(cholesky)/cholesky | solution.py:69
  850.0 95.4 %custom-call.22 = f32[8,128,128]{2,1,0:T(8,128)} custom-call(f32[8,128,128]{2,1,0:T(8,128)} %convolution_subtract_fusion), custom_call_target="Cholesky" | custom-call | tf_op jit(solution)/shard_map/jit(cholesky)/cholesky | solution.py:69
  950.4 5.9 while.12
  956.4 158.7 %custom-call.23 = f32[8,2,128,128]{2,3,1,0:T(8,128)} custom-call(f32[8,2,128,128]{3,2,1,0:T(8,128)} %bitcast.163), custom_call_target="InvertDiagBlocksLowerTriangular" | custom-call | tf_op jit(solution)/shard_map/jit(_cho_solve)/vmap()/triangular_solve | solution.py:70
  1123.5 9.7 all_to_all.33
  1133.3 10.5 gather_fusion
  (250 shorter events, 129.9 us)
Async XLA Ops:
  1.4 5.9 copy-start.12
  1.4 5.9 copy-start.19
  1.4 5.9 copy-start
  7.4 43.3 %copy-start.4 = (f32[4096]{0:T(1024)S(1)}, f32[4096]{0:T(1024)}, u32[]{:S(2)}) copy-start(f32[4096]{0:T(1024)} %param.16) | copy-start | bytes 49156
  7.4 43.3 %copy-start.8 = (f32[4096]{0:T(1024)S(1)}, f32[4096]{0:T(1024)}, u32[]{:S(2)}) copy-start(f32[4096]{0:T(1024)} %param.17) | copy-start | bytes 49156
  50.8 5.9 copy-start.1
  516.5 71.3 %copy-start.23 = (s32[1024]{0:T(1024)S(1)}, s32[1024]{0:T(1024)}, u32[]{:S(2)}) copy-start(s32[1024]{0:T(1024)} %param.13) | copy-start | bytes 12292
  516.5 71.9 %copy-start.24 = (s32[1024]{0:T(1024)S(1)}, s32[1024]{0:T(1024)}, u32[]{:S(2)}) copy-start(s32[1024]{0:T(1024)} %param.12) | copy-start | bytes 12292
  598.6 10.4 all-to-all-start
  609.0 29.0 %all-to-all-start.1 = ((bf16[8,256,256]{2,1,0:T(8,128)(2,1)}), bf16[8,256,256]{2,1,0:T(8,128)(2,1)S(1)}, u32[]{:S(2)}, u32[]{:S(2)}) async-start(bf16[8,256,256]{2,1,0:T(8,128)(2,1)} %bitcast.10), calls=%async_computation.1 | async-start | bytes 2097152 | tf_op jit(solution)/shard_map/all_to_all | solution.py:111
  614.8 23.2 %copy-start.21 = (f32[8]{0:T(128)}, f32[8]{0:T(128)S(1)}, u32[]{:S(2)}) copy-start(f32[8]{0:T(128)S(1)} %iota_convert_fusion) | copy-start | bytes 100
  616.6 21.4 %copy-start.9 = (f32[1,8,256]{2,0,1:T(1,128)}, f32[1,8,256]{2,0,1:T(1,128)S(1)}, u32[]{:S(2)}) copy-start(f32[1,8,256]{2,0,1:T(1,128)S(1)} %get-tuple-element.123) | copy-start | bytes 24580
  668.4 95.8 %copy-start.14 = (pred[128,128]{1,0:T(8,128)(4,1)S(1)}, pred[128,128]{1,0:T(8,128)(4,1)}, u32[]{:S(2)}) copy-start(pred[128,128]{1,0:T(8,128)(4,1)} %iota_compare_fusion.2) | copy-start | bytes 49156
  845.1 100.4 %copy-start.10 = (f32[1,8,256]{2,0,1:T(1,128)S(1)}, f32[1,8,256]{2,0,1:T(1,128)}, u32[]{:S(2)}) copy-start(f32[1,8,256]{2,0,1:T(1,128)} %copy-done.9) | copy-start | bytes 24580
  845.1 100.4 %copy-start.11 = (bf16[2048,8]{0,1:T(8,128)(2,1)S(1)}, bf16[2048,8]{0,1:T(8,128)(2,1)}, u32[]{:S(2)}) copy-start(bf16[2048,8]{0,1:T(8,128)(2,1)} %select_convert_fusion) | copy-start | bytes 98308
  845.1 100.4 %copy-start.15 = (f32[8,256]{1,0:T(8,128)S(1)}, f32[8,256]{1,0:T(8,128)}, u32[]{:S(2)}) copy-start(f32[8,256]{1,0:T(8,128)} %fusion.128) | copy-start | bytes 24580
  845.1 100.4 %copy-start.22 = (f32[8]{0:T(128)S(1)}, f32[8]{0:T(128)}, u32[]{:S(2)}) copy-start(f32[8]{0:T(128)} %copy-done.21) | copy-start | bytes 100
  847.0 98.8 %copy-start.13 = (pred[128,128]{1,0:T(8,128)(4,1)S(1)}, pred[128,128]{1,0:T(8,128)(4,1)}, u32[]{:S(2)}) copy-start(pred[128,128]{1,0:T(8,128)(4,1)} %iota_compare_fusion.3) | copy-start | bytes 49156
  945.7 4.6 copy-start.16
  950.4 164.6 %slice-start = ((f32[8,256,1]{1,0,2:T(8,128)}), f32[8,128,1]{1,0,2:T(8,128)S(1)}, s32[]{:S(2)}) async-start(f32[8,256,1]{1,0,2:T(8,128)} %copy-done.16), calls=%async_computation.3 | async-start | bytes 8192 | tf_op jit(solution)/shard_map/jit(_cho_solve)/vmap()/triangular_solve | solution.py:70
  950.4 167.2 %copy-start.17 = (f32[8,256,1]{1,0,2:T(8,128)S(1)}, f32[8,256,1]{1,0,2:T(8,128)}, u32[]{:S(2)}) copy-start(f32[8,256,1]{1,0,2:T(8,128)} %copy-done.16) | copy-start | bytes 24580
  1115.0 6.8 copy-start.7
  1119.2 14.0 %copy-start.20 = (s32[1024]{0:T(1024)S(1)}, s32[1024]{0:T(1024)}, u32[]{:S(2)}) copy-start(s32[1024]{0:T(1024)} %get-tuple-element.126) | copy-start | bytes 12292
  1122.7 21.1 %copy-start.18 = (f32[8,256]{1,0:T(8,128)}, f32[8,256]{1,0:T(8,128)S(1)}, u32[]{:S(2)}) copy-start(f32[8,256]{1,0:T(8,128)S(1)} %get-tuple-element.95) | copy-start | bytes 24580
  (5 other events, 9.0 us)
